TPU v7x, 32 devices: a whole 2x2x4 slice. The times are simulated.
32 devices in a mesh: tm: 8 (over y, x, core), space: 4 (over z).
Axes of the slice: x: 2, y: 2, z: 4, core: 2. Of those that a mesh axis runs over, the one named last changes fastest.
Arguments:
- start_state: float32 [6, 2048], P(None, 'space'), may hold values from -6 to 6, as said below
- fine_nodes: float32 [8, 3, 6, 2048], P('tm', None, None, 'space'), may hold values from -8 to 8, as said below
Outputs:
- new_places: float32 [8, 3, 3, 2048], P('tm', None, None, 'space')
- new_strengths: float32 [8, 3, 3, 2048], P('tm', None, None, 'space')
- next_places: float32 [8, 3, 2048], P('tm', None, 'space')
- next_strengths: float32 [8, 3, 2048], P('tm', None, 'space')
Inputs may be any that keep to these rules, and one draw needn't show every extreme that they name: `start_state`: rows 0 to 2 are positions within the box from -0.5 to 0.5 give or take 0.05; the particles are numbered along a Morton (Z-order) curve of the box, so that runs of consecutive particles lie close together. `fine_nodes`: rows 0 to 2 are positions within the box from -0.5 to 0.5 give or take 0.1, numbered along the same Morton curve as start_state.
All inputs are finite; a program needn't handle non-finite values.
Results may differ from a plain program's by a relative error of at most 0.0003.
Values sent between devices are 32-bit elements; how exact they have to be, the bound alone decides.
A program may use at most 64 MiB of HBM per device.

v0:
```python
import math

import jax
import jax.numpy as jnp
from jax import lax
from jax.sharding import PartitionSpec as P

CLUSTER = 16


core_squared = 0.01
step_length = 0.02


def from_behind(block, axis, distance):
    devices = range(lax.axis_size(axis))
    route = [(i - distance, i) for i in devices if i - distance in devices]
    return lax.ppermute(block, axis, route)


def cross_rows(left, right):
    return jnp.stack(
        [
            left[1] * right[2] - left[2] * right[1],
            left[2] * right[0] - left[0] * right[2],
            left[0] * right[1] - left[1] * right[0],
        ]
    )


def tile_sums(totals, target, source):
    gap_x = target[0][:, None] - source[0][None, :]
    gap_y = target[1][:, None] - source[1][None, :]
    gap_z = target[2][:, None] - source[2][None, :]
    spread = gap_x * gap_x + gap_y * gap_y + gap_z * gap_z + core_squared
    inverse = lax.rsqrt(spread)
    factor = inverse * inverse * inverse
    steep = 3.0 * factor * inverse * inverse
    curl_x = gap_y * source[5][None, :] - gap_z * source[4][None, :]
    curl_y = gap_z * source[3][None, :] - gap_x * source[5][None, :]
    curl_z = gap_x * source[4][None, :] - gap_y * source[3][None, :]
    along = steep * (
        target[3][:, None] * gap_x + target[4][:, None] * gap_y + target[5][:, None] * gap_z
    )
    velocity = jnp.stack(
        [
            jnp.sum(factor * curl_x, axis=1),
            jnp.sum(factor * curl_y, axis=1),
            jnp.sum(factor * curl_z, axis=1),
        ]
    )
    weighted = jnp.stack(
        [
            jnp.sum(factor * source[3][None, :], axis=1),
            jnp.sum(factor * source[4][None, :], axis=1),
            jnp.sum(factor * source[5][None, :], axis=1),
        ]
    )
    stretch = jnp.stack(
        [
            jnp.sum(along * curl_x, axis=1),
            jnp.sum(along * curl_y, axis=1),
            jnp.sum(along * curl_z, axis=1),
        ]
    )
    return (totals[0] + velocity, totals[1] + weighted, totals[2] + stretch)


def block_sums(totals, target, source):
    length = source.shape[1]
    block_len = math.gcd(length, 512)
    if length == block_len:
        return tile_sums(totals, target, source)
    blocks = source.reshape(6, length // block_len, block_len).transpose(1, 0, 2)

    def scan_step(carry, block):
        return (tile_sums(carry, target, block), None)

    totals, unused = lax.scan(scan_step, totals, blocks)
    return totals


def empty_sums(target):
    zeros = jnp.zeros((3, target.shape[1]), jnp.float32)
    return (zeros, zeros, zeros)


def finish(totals, target, coupling):
    stretch = cross_rows(target[3:6], totals[1]) - totals[2]
    return -coupling * jnp.concatenate([totals[0], stretch], axis=0)


def aggregate(state):
    grouped = state.reshape(6, state.shape[1] // CLUSTER, CLUSTER)
    return jnp.concatenate([jnp.mean(grouped[0:3], axis=2), jnp.sum(grouped[3:6], axis=2)], axis=0)


def shards(start_state, fine_nodes):
    node_states = fine_nodes[0]
    particles_all = start_state.shape[1] * lax.axis_size("space")
    coupling = 1.0 / (4.0 * math.pi * math.sqrt(particles_all))
    is_first = lax.axis_index("tm") == 0

    def evaluate(target, source):
        return finish(block_sums(empty_sums(target), target, source), target, coupling)

    def fine_eval(state):
        totals = block_sums(
            empty_sums(state), state, lax.all_gather(state, "space", axis=1, tiled=True)
        )
        return finish(totals, state, coupling)

    empty = empty_sums(node_states[0])
    totals = (empty, empty, empty, empty, empty)
    column_blocks = (
        lax.all_gather(node_states[0], "space", axis=1, tiled=True),
        lax.all_gather(node_states[1], "space", axis=1, tiled=True),
        lax.all_gather(node_states[2], "space", axis=1, tiled=True),
    )
    fine_first = finish(
        block_sums(totals[0], node_states[0], column_blocks[0]), node_states[0], coupling
    )
    fine_middle = finish(
        block_sums(totals[1], node_states[1], column_blocks[1]), node_states[1], coupling
    )
    fine_last = finish(
        block_sums(totals[2], node_states[2], column_blocks[2]), node_states[2], coupling
    )
    coarse_first = finish(
        block_sums(totals[3], node_states[0], aggregate(column_blocks[0])), node_states[0], coupling
    )
    coarse_last = finish(
        block_sums(totals[4], node_states[2], aggregate(column_blocks[2])), node_states[2], coupling
    )
    correction = step_length * (
        (fine_first + 4.0 * fine_middle + fine_last) / 6.0 - 0.5 * (coarse_first + coarse_last)
    )
    empty_state = jnp.zeros_like(start_state)

    def state_section(section, carry):
        incoming = from_behind(carry[0], "tm", 1)
        initial = jnp.where(is_first, start_state, incoming)
        sources = lax.all_gather(aggregate(initial), "space", axis=1, tiled=True)
        coarse_start = evaluate(initial, sources)
        final_state = (
            initial + step_length * (coarse_start + 0.5 * (coarse_last - coarse_first)) + correction
        )
        return (final_state, initial, coarse_start)

    carry = lax.fori_loop(
        0, lax.axis_size("tm"), state_section, (empty_state, empty_state, empty_state)
    )
    final_state, initial, coarse_start = carry
    last_sources = lax.all_gather(aggregate(final_state), "space", axis=1, tiled=True)
    coarse_end = evaluate(final_state, last_sources)
    change_first = coarse_start - coarse_first
    change_last = coarse_end - coarse_last
    fixed_first = fine_first + change_first
    fixed_middle = fine_middle + 0.5 * (change_first + change_last)
    fixed_last = fine_last + change_last
    slope_first = fine_eval(initial)
    sweep_middle = (
        initial
        + 0.5 * step_length * (slope_first - fixed_first)
        + step_length * (5.0 * fixed_first + 8.0 * fixed_middle - fixed_last) / 24.0
    )
    slope_middle = fine_eval(sweep_middle)
    sweep_last = (
        sweep_middle
        + 0.5 * step_length * (slope_middle - fixed_middle)
        + step_length * (-fixed_first + 8.0 * fixed_middle + 5.0 * fixed_last) / 24.0
    )
    new_nodes = jnp.stack([initial, sweep_middle, sweep_last])[None]
    handed = from_behind(sweep_last, "tm", 1)
    next_start = jnp.where(is_first, start_state, handed)[None]
    return (new_nodes[:, :, 0:3], new_nodes[:, :, 3:6], next_start[:, 0:3], next_start[:, 3:6])


def solution(mesh):
    placed = (P(None, "space"), P("tm", None, None, "space"))
    return jax.shard_map(
        shards,
        mesh=mesh,
        in_specs=placed,
        out_specs=(
            P("tm", None, None, "space"),
            P("tm", None, None, "space"),
            P("tm", None, "space"),
            P("tm", None, "space"),
        ),
        check_vma=False,
    )
```

profile of v0, /device:TPU:4, one launch (start us, length us, event | category | flops | bytes accessed | tf_op | source)
XLA Modules:
  0.0 320.4 jit_solution(13079779013574592536)
XLA Ops:
  1.6 13.5 %all-gather = f32[1,1,6,2048]{3,2,1,0:T(8,128)S(1)} all-gather(f32[1,1,6,512]{3,2,1,0:T(8,128)S(1)} %copy.50), channel_id=2, replica_groups=mesh['tm'=8,'space'=4] {'space'}, dimensions={3}, use_global_device_ids=true | all-gather | bytes 61440 | tf_op jit(solution)/shard_map/all_gather | solution.py:118
  15.6 13.3 %all-gather.1 = f32[1,1,6,2048]{3,2,1,0:T(8,128)S(1)} all-gather(f32[1,1,6,512]{3,2,1,0:T(8,128)S(1)} %copy.49), channel_id=3, replica_groups=mesh['tm'=8,'space'=4] {'space'}, dimensions={3}, use_global_device_ids=true | all-gather | bytes 61440 | tf_op jit(solution)/shard_map/all_gather | solution.py:116
  29.5 10.6 %while.92 = (s32[]{:T(128)}, f32[3,512]{1,0:T(4,128)S(1)}, f32[3,512]{1,0:T(4,128)S(1)}, f32[3,512]{1,0:T(4,128)S(1)}, f32[6,512]{1,0:T(8,128)S(1)}, /*index=5*/...) while((s32[]{:T(128)}, f32[3,512]{1,0:T(4,128)S(1)}, ...), condition=%wide.region_10.11_spmd.clone, body=%wide.region_0.10_spmd.clone.sunk | while | flops 12334600 | bytes 147676 | solution.py:79
  29.5 2.5 fusion.255
  32.2 2.5 fusion.255
  34.8 2.5 fusion.255
  40.1 13.2 %all-gather.2 = f32[1,1,6,2048]{3,2,1,0:T(8,128)S(1)} all-gather(f32[1,1,6,512]{3,2,1,0:T(8,128)S(1)} %copy.51), channel_id=4, replica_groups=mesh['tm'=8,'space'=4] {'space'}, dimensions={3}, use_global_device_ids=true | all-gather | bytes 61440 | tf_op jit(solution)/shard_map/all_gather | solution.py:117
  53.3 10.5 %while.93 = (s32[]{:T(128)}, f32[3,512]{1,0:T(4,128)S(1)}, f32[3,512]{1,0:T(4,128)S(1)}, f32[3,512]{1,0:T(4,128)S(1)}, f32[6,512]{1,0:T(8,128)S(1)}, /*index=5*/...) while((s32[]{:T(128)}, f32[3,512]{1,0:T(4,128)S(1)}, ...), condition=%wide.region_21.22_spmd.clone, body=%wide.region_11.21_spmd.clone.sunk | while | flops 12334600 | bytes 147676 | solution.py:79
  63.9 10.6 %while.94 = (s32[]{:T(128)}, f32[3,512]{1,0:T(4,128)S(1)}, f32[3,512]{1,0:T(4,128)S(1)}, f32[3,512]{1,0:T(4,128)S(1)}, f32[6,512]{1,0:T(8,128)S(1)}, /*index=5*/...) while((s32[]{:T(128)}, f32[3,512]{1,0:T(4,128)S(1)}, ...), condition=%wide.region_32.33_spmd.clone, body=%wide.region_22.32_spmd.clone.sunk | while | flops 12334600 | bytes 147676 | solution.py:79
  77.7 172.0 %while.95 = (s32[]{:T(128)}, f32[6,512]{1,0:T(8,128)S(1)}, f32[6,512]{1,0:T(8,128)}, f32[6,512]{1,0:T(8,128)}, pred[]{:T(512)}, /*index=5*/f32[6,512]{1,0:T(8,12...) while((s32[]{:T(128)}, f32[6,512]{1,0:T(8,128)S(1)}, ...), condition=%wide.region_67.68_spmd.clone, body=%wide.region_55.67_spmd.clone.sunk | while | flops 3124835 | bytes 415684 | solution.py:150
  79.6 4.0 %collective-permute-done = f32[6,512]{1,0:T(8,128)S(1)} collective-permute-done((f32[6,512]{1,0:T(8,128)S(1)}, f32[6,512]{1,0:T(8,128)S(1)}, u32[]{:S(2)}, u32[]{:S(2)}) %collective-permute-start) | collective-permute-done | bytes 12320 | tf_op jit(solution)/shard_map/while/body/eval_jaxpr/ppermute | solution.py:18
  84.0 13.2 %all-gather.7 = f32[4,32,6]{1,2,0:T(8,128)S(1)} all-gather(f32[1,32,6]{1,2,0:T(8,128)S(1)} %maximum_bitcast_fusion.4), channel_id=1, replica_groups=mesh['tm'=8,'space'=4] {'space'}, dimensions={0}, use_global_device_ids=true | all-gather | bytes 3840 | tf_op jit(solution)/shard_map/while/body/eval_jaxpr/all_gather | solution.py:143
  101.1 4.0 %collective-permute-done = f32[6,512]{1,0:T(8,128)S(1)} collective-permute-done((f32[6,512]{1,0:T(8,128)S(1)}, f32[6,512]{1,0:T(8,128)S(1)}, u32[]{:S(2)}, u32[]{:S(2)}) %collective-permute-start) | collective-permute-done | bytes 12320 | tf_op jit(solution)/shard_map/while/body/eval_jaxpr/ppermute | solution.py:18
  105.5 13.2 %all-gather.7 = f32[4,32,6]{1,2,0:T(8,128)S(1)} all-gather(f32[1,32,6]{1,2,0:T(8,128)S(1)} %maximum_bitcast_fusion.4), channel_id=1, replica_groups=mesh['tm'=8,'space'=4] {'space'}, dimensions={0}, use_global_device_ids=true | all-gather | bytes 3840 | tf_op jit(solution)/shard_map/while/body/eval_jaxpr/all_gather | solution.py:143
  122.6 4.0 %collective-permute-done = f32[6,512]{1,0:T(8,128)S(1)} collective-permute-done((f32[6,512]{1,0:T(8,128)S(1)}, f32[6,512]{1,0:T(8,128)S(1)}, u32[]{:S(2)}, u32[]{:S(2)}) %collective-permute-start) | collective-permute-done | bytes 12320 | tf_op jit(solution)/shard_map/while/body/eval_jaxpr/ppermute | solution.py:18
  127.0 13.2 %all-gather.7 = f32[4,32,6]{1,2,0:T(8,128)S(1)} all-gather(f32[1,32,6]{1,2,0:T(8,128)S(1)} %maximum_bitcast_fusion.4), channel_id=1, replica_groups=mesh['tm'=8,'space'=4] {'space'}, dimensions={0}, use_global_device_ids=true | all-gather | bytes 3840 | tf_op jit(solution)/shard_map/while/body/eval_jaxpr/all_gather | solution.py:143
  144.1 4.0 %collective-permute-done = f32[6,512]{1,0:T(8,128)S(1)} collective-permute-done((f32[6,512]{1,0:T(8,128)S(1)}, f32[6,512]{1,0:T(8,128)S(1)}, u32[]{:S(2)}, u32[]{:S(2)}) %collective-permute-start) | collective-permute-done | bytes 12320 | tf_op jit(solution)/shard_map/while/body/eval_jaxpr/ppermute | solution.py:18
  148.6 13.2 %all-gather.7 = f32[4,32,6]{1,2,0:T(8,128)S(1)} all-gather(f32[1,32,6]{1,2,0:T(8,128)S(1)} %maximum_bitcast_fusion.4), channel_id=1, replica_groups=mesh['tm'=8,'space'=4] {'space'}, dimensions={0}, use_global_device_ids=true | all-gather | bytes 3840 | tf_op jit(solution)/shard_map/while/body/eval_jaxpr/all_gather | solution.py:143
  165.6 4.0 %collective-permute-done = f32[6,512]{1,0:T(8,128)S(1)} collective-permute-done((f32[6,512]{1,0:T(8,128)S(1)}, f32[6,512]{1,0:T(8,128)S(1)}, u32[]{:S(2)}, u32[]{:S(2)}) %collective-permute-start) | collective-permute-done | bytes 12320 | tf_op jit(solution)/shard_map/while/body/eval_jaxpr/ppermute | solution.py:18
  170.1 13.2 %all-gather.7 = f32[4,32,6]{1,2,0:T(8,128)S(1)} all-gather(f32[1,32,6]{1,2,0:T(8,128)S(1)} %maximum_bitcast_fusion.4), channel_id=1, replica_groups=mesh['tm'=8,'space'=4] {'space'}, dimensions={0}, use_global_device_ids=true | all-gather | bytes 3840 | tf_op jit(solution)/shard_map/while/body/eval_jaxpr/all_gather | solution.py:143
  187.1 4.0 %collective-permute-done = f32[6,512]{1,0:T(8,128)S(1)} collective-permute-done((f32[6,512]{1,0:T(8,128)S(1)}, f32[6,512]{1,0:T(8,128)S(1)}, u32[]{:S(2)}, u32[]{:S(2)}) %collective-permute-start) | collective-permute-done | bytes 12320 | tf_op jit(solution)/shard_map/while/body/eval_jaxpr/ppermute | solution.py:18
  191.6 13.2 %all-gather.7 = f32[4,32,6]{1,2,0:T(8,128)S(1)} all-gather(f32[1,32,6]{1,2,0:T(8,128)S(1)} %maximum_bitcast_fusion.4), channel_id=1, replica_groups=mesh['tm'=8,'space'=4] {'space'}, dimensions={0}, use_global_device_ids=true | all-gather | bytes 3840 | tf_op jit(solution)/shard_map/while/body/eval_jaxpr/all_gather | solution.py:143
  208.6 4.0 %collective-permute-done = f32[6,512]{1,0:T(8,128)S(1)} collective-permute-done((f32[6,512]{1,0:T(8,128)S(1)}, f32[6,512]{1,0:T(8,128)S(1)}, u32[]{:S(2)}, u32[]{:S(2)}) %collective-permute-start) | collective-permute-done | bytes 12320 | tf_op jit(solution)/shard_map/while/body/eval_jaxpr/ppermute | solution.py:18
  213.1 13.2 %all-gather.7 = f32[4,32,6]{1,2,0:T(8,128)S(1)} all-gather(f32[1,32,6]{1,2,0:T(8,128)S(1)} %maximum_bitcast_fusion.4), channel_id=1, replica_groups=mesh['tm'=8,'space'=4] {'space'}, dimensions={0}, use_global_device_ids=true | all-gather | bytes 3840 | tf_op jit(solution)/shard_map/while/body/eval_jaxpr/all_gather | solution.py:143
  230.1 4.0 %collective-permute-done = f32[6,512]{1,0:T(8,128)S(1)} collective-permute-done((f32[6,512]{1,0:T(8,128)S(1)}, f32[6,512]{1,0:T(8,128)S(1)}, u32[]{:S(2)}, u32[]{:S(2)}) %collective-permute-start) | collective-permute-done | bytes 12320 | tf_op jit(solution)/shard_map/while/body/eval_jaxpr/ppermute | solution.py:18
  234.6 13.2 %all-gather.7 = f32[4,32,6]{1,2,0:T(8,128)S(1)} all-gather(f32[1,32,6]{1,2,0:T(8,128)S(1)} %maximum_bitcast_fusion.4), channel_id=1, replica_groups=mesh['tm'=8,'space'=4] {'space'}, dimensions={0}, use_global_device_ids=true | all-gather | bytes 3840 | tf_op jit(solution)/shard_map/while/body/eval_jaxpr/all_gather | solution.py:143
  250.2 13.2 %all-gather.4 = f32[4,32,6]{1,2,0:T(8,128)S(1)} all-gather(f32[1,32,6]{1,2,0:T(8,128)S(1)} %maximum_bitcast_fusion.2), channel_id=1, replica_groups=mesh['tm'=8,'space'=4] {'space'}, dimensions={0}, use_global_device_ids=true | all-gather | bytes 3840 | tf_op jit(solution)/shard_map/all_gather | solution.py:154
  264.1 13.4 %all_gather.26 = f32[6,2048]{1,0:T(8,128)S(1)} all-gather(f32[6,512]{1,0:T(8,128)S(1)} %copy-done.1), channel_id=1, replica_groups=mesh['tm'=8,'space'=4] {'space'}, dimensions={1}, use_global_device_ids=true | all-gather | bytes 61440 | tf_op jit(solution)/shard_map/all_gather | solution.py:109
  277.5 10.5 %while.96 = (s32[]{:T(128)}, f32[3,512]{1,0:T(4,128)S(1)}, f32[3,512]{1,0:T(4,128)S(1)}, f32[3,512]{1,0:T(4,128)S(1)}, f32[6,512]{1,0:T(8,128)S(1)}, /*index=5*/...) while((s32[]{:T(128)}, f32[3,512]{1,0:T(4,128)S(1)}, ...), condition=%wide.region_78.79_spmd.clone, body=%wide.region_68.78_spmd.clone.sunk | while | flops 12334600 | bytes 147676 | solution.py:79
  290.0 13.1 %all_gather.28 = f32[6,2048]{1,0:T(8,128)S(1)} all-gather(f32[6,512]{1,0:T(8,128)S(1)} %fusion.201), channel_id=1, replica_groups=mesh['tm'=8,'space'=4] {'space'}, dimensions={1}, use_global_device_ids=true | all-gather | bytes 61440 | tf_op jit(solution)/shard_map/all_gather | solution.py:109
  303.1 10.5 %while.97 = (s32[]{:T(128)}, f32[3,512]{1,0:T(4,128)S(1)}, f32[3,512]{1,0:T(4,128)S(1)}, f32[3,512]{1,0:T(4,128)S(1)}, f32[6,512]{1,0:T(8,128)S(1)}, /*index=5*/...) while((s32[]{:T(128)}, f32[3,512]{1,0:T(4,128)S(1)}, ...), condition=%wide.region_100.101_spmd.clone, body=%wide.region_90.100_spmd.clone.sunk | while | flops 12334600 | bytes 147676 | solution.py:79
  317.0 2.7 collective-permute-done.1
  (342 shorter events, 90.0 us)
Async XLA Ops:
  0.6 0.8 copy-start.3
  76.9 0.7 copy-start.2
  77.7 5.9 %collective-permute-start = (f32[6,512]{1,0:T(8,128)S(1)}, f32[6,512]{1,0:T(8,128)S(1)}, u32[]{:S(2)}, u32[]{:S(2)}) collective-permute-start(f32[6,512]{1,0:T(8,128)S(1)} %broadcast_select_fusion.5), channel_id=1, source_target_pairs={{0,4},{4,8},{8,12},{12,16},{16,20},{20,24},{24,28},{1,5},{5,9},{9,... | collective-permute-start | bytes 36872 | tf_op jit(solution)/shard_map/while/body/eval_jaxpr/ppermute | solution.py:18
  83.6 14.9 %copy-start = (f32[6,512]{1,0:T(8,128)}, f32[6,512]{1,0:T(8,128)S(1)}, u32[]{:S(2)}) copy-start(f32[6,512]{1,0:T(8,128)S(1)} %broadcast_select_fusion.6) | copy-start | bytes 36868 | tf_op jit(solution)/shard_map/while
  99.2 5.9 %collective-permute-start = (f32[6,512]{1,0:T(8,128)S(1)}, f32[6,512]{1,0:T(8,128)S(1)}, u32[]{:S(2)}, u32[]{:S(2)}) collective-permute-start(f32[6,512]{1,0:T(8,128)S(1)} %broadcast_select_fusion.5), channel_id=1, source_target_pairs={{0,4},{4,8},{8,12},{12,16},{16,20},{20,24},{24,28},{1,5},{5,9},{9,... | collective-permute-start | bytes 36872 | tf_op jit(solution)/shard_map/while/body/eval_jaxpr/ppermute | solution.py:18
  105.1 14.9 %copy-start = (f32[6,512]{1,0:T(8,128)}, f32[6,512]{1,0:T(8,128)S(1)}, u32[]{:S(2)}) copy-start(f32[6,512]{1,0:T(8,128)S(1)} %broadcast_select_fusion.6) | copy-start | bytes 36868 | tf_op jit(solution)/shard_map/while
  120.7 5.9 %collective-permute-start = (f32[6,512]{1,0:T(8,128)S(1)}, f32[6,512]{1,0:T(8,128)S(1)}, u32[]{:S(2)}, u32[]{:S(2)}) collective-permute-start(f32[6,512]{1,0:T(8,128)S(1)} %broadcast_select_fusion.5), channel_id=1, source_target_pairs={{0,4},{4,8},{8,12},{12,16},{16,20},{20,24},{24,28},{1,5},{5,9},{9,... | collective-permute-start | bytes 36872 | tf_op jit(solution)/shard_map/while/body/eval_jaxpr/ppermute | solution.py:18
  126.6 14.9 %copy-start = (f32[6,512]{1,0:T(8,128)}, f32[6,512]{1,0:T(8,128)S(1)}, u32[]{:S(2)}) copy-start(f32[6,512]{1,0:T(8,128)S(1)} %broadcast_select_fusion.6) | copy-start | bytes 36868 | tf_op jit(solution)/shard_map/while
  142.2 5.9 %collective-permute-start = (f32[6,512]{1,0:T(8,128)S(1)}, f32[6,512]{1,0:T(8,128)S(1)}, u32[]{:S(2)}, u32[]{:S(2)}) collective-permute-start(f32[6,512]{1,0:T(8,128)S(1)} %broadcast_select_fusion.5), channel_id=1, source_target_pairs={{0,4},{4,8},{8,12},{12,16},{16,20},{20,24},{24,28},{1,5},{5,9},{9,... | collective-permute-start | bytes 36872 | tf_op jit(solution)/shard_map/while/body/eval_jaxpr/ppermute | solution.py:18
  148.1 14.9 %copy-start = (f32[6,512]{1,0:T(8,128)}, f32[6,512]{1,0:T(8,128)S(1)}, u32[]{:S(2)}) copy-start(f32[6,512]{1,0:T(8,128)S(1)} %broadcast_select_fusion.6) | copy-start | bytes 36868 | tf_op jit(solution)/shard_map/while
  163.7 5.9 %collective-permute-start = (f32[6,512]{1,0:T(8,128)S(1)}, f32[6,512]{1,0:T(8,128)S(1)}, u32[]{:S(2)}, u32[]{:S(2)}) collective-permute-start(f32[6,512]{1,0:T(8,128)S(1)} %broadcast_select_fusion.5), channel_id=1, source_target_pairs={{0,4},{4,8},{8,12},{12,16},{16,20},{20,24},{24,28},{1,5},{5,9},{9,... | collective-permute-start | bytes 36872 | tf_op jit(solution)/shard_map/while/body/eval_jaxpr/ppermute | solution.py:18
  169.6 14.9 %copy-start = (f32[6,512]{1,0:T(8,128)}, f32[6,512]{1,0:T(8,128)S(1)}, u32[]{:S(2)}) copy-start(f32[6,512]{1,0:T(8,128)S(1)} %broadcast_select_fusion.6) | copy-start | bytes 36868 | tf_op jit(solution)/shard_map/while
  185.2 5.9 %collective-permute-start = (f32[6,512]{1,0:T(8,128)S(1)}, f32[6,512]{1,0:T(8,128)S(1)}, u32[]{:S(2)}, u32[]{:S(2)}) collective-permute-start(f32[6,512]{1,0:T(8,128)S(1)} %broadcast_select_fusion.5), channel_id=1, source_target_pairs={{0,4},{4,8},{8,12},{12,16},{16,20},{20,24},{24,28},{1,5},{5,9},{9,... | collective-permute-start | bytes 36872 | tf_op jit(solution)/shard_map/while/body/eval_jaxpr/ppermute | solution.py:18
  191.1 14.9 %copy-start = (f32[6,512]{1,0:T(8,128)}, f32[6,512]{1,0:T(8,128)S(1)}, u32[]{:S(2)}) copy-start(f32[6,512]{1,0:T(8,128)S(1)} %broadcast_select_fusion.6) | copy-start | bytes 36868 | tf_op jit(solution)/shard_map/while
  206.7 5.9 %collective-permute-start = (f32[6,512]{1,0:T(8,128)S(1)}, f32[6,512]{1,0:T(8,128)S(1)}, u32[]{:S(2)}, u32[]{:S(2)}) collective-permute-start(f32[6,512]{1,0:T(8,128)S(1)} %broadcast_select_fusion.5), channel_id=1, source_target_pairs={{0,4},{4,8},{8,12},{12,16},{16,20},{20,24},{24,28},{1,5},{5,9},{9,... | collective-permute-start | bytes 36872 | tf_op jit(solution)/shard_map/while/body/eval_jaxpr/ppermute | solution.py:18
  212.6 14.9 %copy-start = (f32[6,512]{1,0:T(8,128)}, f32[6,512]{1,0:T(8,128)S(1)}, u32[]{:S(2)}) copy-start(f32[6,512]{1,0:T(8,128)S(1)} %broadcast_select_fusion.6) | copy-start | bytes 36868 | tf_op jit(solution)/shard_map/while
  228.2 5.9 %collective-permute-start = (f32[6,512]{1,0:T(8,128)S(1)}, f32[6,512]{1,0:T(8,128)S(1)}, u32[]{:S(2)}, u32[]{:S(2)}) collective-permute-start(f32[6,512]{1,0:T(8,128)S(1)} %broadcast_select_fusion.5), channel_id=1, source_target_pairs={{0,4},{4,8},{8,12},{12,16},{16,20},{20,24},{24,28},{1,5},{5,9},{9,... | collective-permute-start | bytes 36872 | tf_op jit(solution)/shard_map/while/body/eval_jaxpr/ppermute | solution.py:18
  234.1 14.9 %copy-start = (f32[6,512]{1,0:T(8,128)}, f32[6,512]{1,0:T(8,128)S(1)}, u32[]{:S(2)}) copy-start(f32[6,512]{1,0:T(8,128)S(1)} %broadcast_select_fusion.6) | copy-start | bytes 36868 | tf_op jit(solution)/shard_map/while
  263.4 0.7 copy-start.1
  289.2 0.7 copy-start.4
  313.8 6.0 %collective-permute-start.1 = (f32[6,512]{1,0:T(8,128)S(1)}, f32[6,512]{1,0:T(8,128)S(1)}, u32[]{:S(2)}, u32[]{:S(2)}) collective-permute-start(f32[6,512]{1,0:T(8,128)S(1)} %fusion.206), channel_id=1, source_target_pairs={{0,4},{4,8},{8,12},{12,16},{16,20},{20,24},{24,28},{1,5},{5,9},{9,... | collective-permute-start | bytes 36872 | tf_op jit(solution)/shard_map/ppermute | solution.py:18
where the time goes:
time: 321 us; the launch traced here: 320 us
  blocking collectives  185 us (58%)
  other arithmetic  71.9 us (22%)
  waiting for transfers between devices  35 us (11%)
  starting transfers between devices  17.2 us (5%)
  local copies, waits for them, and re-layouts  8.51 us (3%)
    all_gather x8, blocking collectives, state_section(): sources = lax.all_gather(aggregate(initial), 'space', axis=1, tiled=True)  106 us
    reduce_sum x31, other arithmetic, tile_sums(): jnp.sum(along * curl_x, axis=1)  62.7 us
    ppermute x9, waiting for transfers between devices, from_behind(): return lax.ppermute(block, axis, route)  35 us
    all_gather x2, blocking collectives, fine_eval(): lax.all_gather(state, 'space', axis=1, tiled=True)  26.5 us
    ppermute x9, starting transfers between devices, from_behind(): return lax.ppermute(block, axis, route)  17.2 us
    all_gather x1, blocking collectives, shards(): lax.all_gather(node_states[2], 'space', axis=1, tiled=True)  13.5 us
    all_gather x1, blocking collectives, shards(): lax.all_gather(node_states[0], 'space', axis=1, tiled=True)  13.3 us
    all_gather x1, blocking collectives, shards(): lax.all_gather(aggregate(final_state), 'space', axis=1, tiled=True)  13.2 us
  transfers between devices with their start and end apart: 9, of which 9 were waited for; matrix products, arithmetic and copies ran while one was open for 0% of the time, Pallas kernels for 0%

commit v1 on v0

v1 whole, which is shorter than its diff:
```python
import functools
import math

import jax
import jax.numpy as jnp
from jax import lax
from jax.experimental import pallas as pl
from jax.experimental.pallas import tpu as pltpu
from jax.sharding import PartitionSpec as P

CLUSTER = 16

core_squared = 0.01
step_length = 0.02


def rounded(value):
    return value.astype(jnp.bfloat16).astype(jnp.float32)


def split_three(value):
    one = rounded(value)
    two = rounded(value - one)
    return one, two, rounded(value - one - two)


def split_two(value):
    high = value.astype(jnp.bfloat16)
    return high, (value - high.astype(jnp.float32)).astype(jnp.bfloat16)


def product(left, right):
    return jnp.dot(left, right, preferred_element_type=jnp.float32)


def pad_rows(value):
    return jnp.concatenate([value, jnp.zeros((8 - value.shape[0], value.shape[1]), value.dtype)], axis=0)


def place_parts(state, extra):
    high = rounded(state[0:3])
    low = rounded(state[0:3] - high)
    used = high + low
    norm = used[0:1] * used[0:1] + used[1:2] * used[1:2] + used[2:3] * used[2:3] + extra
    return high, low, split_three(norm)


def source_places(state):
    high, low, norm = place_parts(state, 0.0)
    ones = jnp.ones_like(norm[0])
    none = jnp.zeros_like(norm[0])
    return jnp.concatenate(
        [high, norm[0], norm[1], norm[2], ones, ones]
        + [low, ones, none, none, none, none]
        + [high, none, none, none, none, none]
        + [low, none, none, none, none, none],
        axis=0,
    ).astype(jnp.bfloat16)


def target_places(state):
    high, low, norm = place_parts(state, core_squared)
    high = -2.0 * high
    low = -2.0 * low
    ones = jnp.ones_like(norm[0])
    none = jnp.zeros_like(norm[0])
    return jnp.concatenate(
        [high, ones, ones, ones, norm[0], norm[1]]
        + [high, norm[2], none, none, none, none]
        + [low, none, none, none, none, none]
        + [low, none, none, none, none, none],
        axis=0,
    ).astype(jnp.bfloat16)


def cross(left, right):
    return jnp.concatenate(
        [
            left[1:2] * right[2:3] - left[2:3] * right[1:2],
            left[2:3] * right[0:1] - left[0:1] * right[2:3],
            left[0:1] * right[1:2] - left[1:2] * right[0:1],
        ],
        axis=0,
    )


def source_moments(state):
    base = pad_rows(jnp.concatenate([state[3:6], cross(state[0:3], state[3:6])], axis=0))
    whole = jnp.concatenate([base, state[0:1] * base, state[1:2] * base, state[2:3] * base], axis=0)
    high = rounded(whole)
    low = whole - high
    for_q = jnp.concatenate([high[0:8], low[0:8]], axis=0).astype(jnp.bfloat16)
    for_h = jnp.concatenate([high, low], axis=0).astype(jnp.bfloat16)
    return for_q, for_h


def pair_sums(places, for_q, for_h, target):
    count = target.shape[1]
    sum_q = jnp.zeros((8, count), jnp.float32)
    sum_h = jnp.zeros((32, count), jnp.float32)
    length = places.shape[1]
    piece = math.gcd(length, 256)
    for begin in range(0, length, piece):
        part = slice(begin, begin + piece)
        spread = lax.dot_general(
            places[:, part], target, (((0,), (0,)), ((), ())), preferred_element_type=jnp.float32
        )
        inverse = lax.rsqrt(spread)
        square = inverse * inverse
        factor = square * inverse
        steep = factor * square
        factor_high, factor_low = split_two(factor)
        steep_high, steep_low = split_two(steep)
        got_q = product(for_q[:, part], factor_high) + product(for_q[:, part], factor_low)
        got_h = product(for_h[:, part], steep_high)
        low_h = product(for_h[0:32, part], steep_low)
        sum_q = sum_q + (got_q[0:8] + got_q[8:16])
        sum_h = sum_h + (got_h[0:32] + got_h[32:64] + low_h)
    return jnp.concatenate([sum_q, sum_h], axis=0)


def finish(sums, state, coupling):
    places = state[0:3]
    strengths = state[3:6]
    weighted = sums[0:3]
    velocity = cross(places, weighted) - sums[3:6]
    along = (
        strengths[0:1] * places[0:1] + strengths[1:2] * places[1:2] + strengths[2:3] * places[2:3]
    )
    moment = 3.0 * (
        along * sums[8:16]
        - strengths[0:1] * sums[16:24]
        - strengths[1:2] * sums[24:32]
        - strengths[2:3] * sums[32:40]
    )
    stretch = cross(strengths, weighted) - (cross(places, moment[0:3]) - moment[3:6])
    return -coupling * jnp.concatenate([velocity, stretch], axis=0)


def kernel(
    n_t,
    n_s,
    start_ref,
    nodes_ref,
    places_out,
    strengths_out,
    next_places_out,
    next_strengths_out,
    gathered,
    sums,
    steps,
    history,
    coarse,
    middles,
    handed,
    pool,
    send_a,
    recv_a,
    send_b,
    recv_b,
    send_d,
    recv_d,
    send_e,
    recv_e,
    send_w,
    recv_w,
    send_h,
    recv_h,
):
    length = start_ref.shape[1]
    coupling = 1.0 / (4.0 * math.pi * math.sqrt(length * n_s))
    mine = lax.axis_index("tm")
    me = lax.axis_index("space")

    def space_copy(source, target, send, recv, peer):
        return pltpu.make_async_remote_copy(
            src_ref=source, dst_ref=target, send_sem=send, recv_sem=recv,
            device_id={"space": peer}, device_id_type=pl.DeviceIdType.MESH,
        )

    def time_copy(source, target, send, recv, peer):
        return pltpu.make_async_remote_copy(
            src_ref=source, dst_ref=target, send_sem=send, recv_sem=recv,
            device_id={"tm": peer}, device_id_type=pl.DeviceIdType.MESH,
        )

    barrier = pltpu.get_barrier_semaphore()
    for offset in range(1, n_s):
        pl.semaphore_signal(
            barrier, inc=1, device_id={"space": lax.rem(me + offset, n_s)},
            device_id_type=pl.DeviceIdType.MESH,
        )
    for offset in range(1, n_t):
        pl.semaphore_signal(
            barrier, inc=1, device_id={"tm": lax.rem(mine + offset, n_t)},
            device_id_type=pl.DeviceIdType.MESH,
        )
    pl.semaphore_wait(barrier, n_s - 1 + n_t - 1)

    def node_copy(offset, slot):
        return space_copy(
            nodes_ref.at[0], gathered.at[slot], send_a.at[offset], recv_a.at[offset],
            lax.rem(me + offset, n_s),
        )

    def start_copy(offset, slot):
        return space_copy(
            start_ref, history.at[0, slot], send_b.at[offset], recv_b.at[offset],
            lax.rem(me + offset, n_s),
        )

    for offset in range(1, n_s):
        node_copy(offset, me).start()
    for offset in range(1, n_s):
        start_copy(offset, me).start()
    gathered[me] = nodes_ref[0]
    history[0, me] = start_ref[...]

    total = n_s * length
    clusters = total // CLUSTER
    particle = lax.broadcasted_iota(jnp.int32, (total, clusters), 0)
    cluster = lax.broadcasted_iota(jnp.int32, (total, clusters), 1)
    offset_in = particle - cluster * CLUSTER
    pool[...] = jnp.where((offset_in >= 0) & (offset_in < CLUSTER), 1.0, 0.0).astype(jnp.bfloat16)

    def aggregate(blocks):
        state = pad_rows(jnp.concatenate(blocks, axis=1))
        parts = jnp.concatenate(split_three(state), axis=0).astype(jnp.bfloat16)
        got = jnp.dot(parts, pool[...], preferred_element_type=jnp.float32)
        whole = got[0:8] + got[8:16] + got[16:24]
        return jnp.concatenate([whole[0:3] * (1.0 / CLUSTER), whole[3:6]], axis=0)

    def coarse_sources(blocks):
        merged = aggregate(blocks)
        return (source_places(merged),) + source_moments(merged)

    def fine_sums(source, target):
        for_q, for_h = source_moments(source)
        return pair_sums(source_places(source), for_q, for_h, target_places(target))

    for offset in range(n_s):
        source = lax.rem(me + n_s - offset, n_s)
        if offset > 0:
            node_copy(offset, source).wait_recv()

        def one_node(node, carry):
            got = fine_sums(gathered[source, node], nodes_ref[0, node])
            if offset == 0:
                sums[node] = got
            else:
                sums[node] = sums[node] + got
            return carry

        lax.fori_loop(0, 3, one_node, 0)

    fine = [finish(sums[node], nodes_ref[0, node], coupling) for node in range(3)]

    def coarse_value(blocks, target):
        return finish(pair_sums(*coarse_sources(blocks), target_places(target)), target, coupling)

    coarse_first = coarse_value([gathered[z, 0] for z in range(n_s)], nodes_ref[0, 0])
    coarse_last = coarse_value([gathered[z, 2] for z in range(n_s)], nodes_ref[0, 2])
    correction = step_length * (
        (fine[0] + 4.0 * fine[1] + fine[2]) / 6.0 - 0.5 * (coarse_first + coarse_last)
    )
    steps[mine, me] = correction + step_length * 0.5 * (coarse_last - coarse_first)

    def step_copy(offset, slot):
        return space_copy(
            steps.at[mine, me], steps.at[mine, slot], send_d.at[offset], recv_d.at[offset],
            lax.rem(me + offset, n_s),
        )

    for offset in range(1, n_s):
        step_copy(offset, me).start()
    for offset in range(1, n_s):
        start_copy(offset, lax.rem(me + n_s - offset, n_s)).wait_recv()
    for offset in range(1, n_s):
        step_copy(offset, lax.rem(me + n_s - offset, n_s)).wait_recv()

    def slice_copy(offset, slot):
        return time_copy(
            steps.at[slot], steps.at[slot], send_e.at[offset], recv_e.at[offset],
            lax.rem(mine + offset, n_t),
        )

    for offset in range(1, n_t):
        slice_copy(offset, mine).start()

    def chain_step(step, carry):
        sources = coarse_sources([history[step, z] for z in range(n_s)])

        @pl.when(step != mine)
        def _():
            slice_copy(lax.rem(mine + n_t - step, n_t), step).wait_recv()

        def one_block(z, inner):
            state = history[step, z]
            value = finish(pair_sums(*sources, target_places(state)), state, coupling)
            coarse[step, z] = value
            history[step + 1, z] = state + step_length * value + steps[step, z]
            return inner

        lax.fori_loop(0, n_s, one_block, 0, unroll=math.gcd(n_s, 4))
        return carry

    lax.fori_loop(0, n_t, chain_step, 0)

    initial = history[mine, me]
    final_state = history[mine + 1, me]
    coarse_end = coarse_value([history[mine + 1, z] for z in range(n_s)], final_state)
    change_first = coarse[mine, me] - coarse_first
    change_last = coarse_end - coarse_last
    fixed_first = fine[0] + change_first
    fixed_middle = fine[1] + 0.5 * (change_first + change_last)
    fixed_last = fine[2] + change_last

    sums[0] = jnp.zeros(sums.shape[1:], jnp.float32)

    def initial_block(z, carry):
        sums[0] = sums[0] + fine_sums(history[mine, z], history[mine, me])
        return carry

    lax.fori_loop(0, n_s, initial_block, 0)
    slope_first = finish(sums[0], initial, coupling)
    sweep_middle = (
        initial
        + 0.5 * step_length * (slope_first - fixed_first)
        + step_length * (5.0 * fixed_first + 8.0 * fixed_middle - fixed_last) / 24.0
    )
    middles[me] = sweep_middle

    def middle_copy(offset, slot):
        return space_copy(
            middles.at[me], middles.at[slot], send_w.at[offset], recv_w.at[offset],
            lax.rem(me + offset, n_s),
        )

    for offset in range(1, n_s):
        middle_copy(offset, me).start()
    places_out[0, 0] = initial[0:3]
    strengths_out[0, 0] = initial[3:6]
    places_out[0, 1] = sweep_middle[0:3]
    strengths_out[0, 1] = sweep_middle[3:6]
    sums[1] = fine_sums(sweep_middle, sweep_middle)
    for offset in range(1, n_s):
        source = lax.rem(me + n_s - offset, n_s)
        middle_copy(offset, source).wait_recv()
        sums[1] = sums[1] + fine_sums(middles[source], sweep_middle)
    slope_middle = finish(sums[1], sweep_middle, coupling)
    sweep_last = (
        sweep_middle
        + 0.5 * step_length * (slope_middle - fixed_middle)
        + step_length * (-fixed_first + 8.0 * fixed_middle + 5.0 * fixed_last) / 24.0
    )
    handed[0] = sweep_last

    def last_copy():
        return time_copy(handed.at[0], handed.at[1], send_h, recv_h, lax.rem(mine + 1, n_t))

    @pl.when(mine < n_t - 1)
    def _():
        last_copy().start()

    places_out[0, 2] = sweep_last[0:3]
    strengths_out[0, 2] = sweep_last[3:6]
    for offset in range(1, n_s):
        node_copy(offset, me).wait_send()
        start_copy(offset, me).wait_send()
        step_copy(offset, me).wait_send()
        middle_copy(offset, me).wait_send()
    for offset in range(1, n_t):
        slice_copy(offset, mine).wait_send()

    @pl.when(mine == 0)
    def _():
        next_places_out[0] = start_ref[0:3]
        next_strengths_out[0] = start_ref[3:6]

    @pl.when(mine > 0)
    def _():
        last_copy().wait_recv()
        next_places_out[0] = handed[1, 0:3]
        next_strengths_out[0] = handed[1, 3:6]

    @pl.when(mine < n_t - 1)
    def _():
        last_copy().wait_send()


def solution(mesh):
    n_t, n_s = mesh.shape["tm"], mesh.shape["space"]

    def shards(start_state, fine_nodes):
        length = start_state.shape[1]
        total = length * n_s
        vmem = pl.BlockSpec(memory_space=pltpu.VMEM)
        dma = pltpu.SemaphoreType.DMA
        return pl.pallas_call(
            functools.partial(kernel, n_t, n_s),
            out_shape=(
                jax.ShapeDtypeStruct((1, 3, 3, length), jnp.float32),
                jax.ShapeDtypeStruct((1, 3, 3, length), jnp.float32),
                jax.ShapeDtypeStruct((1, 3, length), jnp.float32),
                jax.ShapeDtypeStruct((1, 3, length), jnp.float32),
            ),
            in_specs=[vmem, vmem],
            out_specs=(vmem, vmem, vmem, vmem),
            scratch_shapes=[
                pltpu.VMEM((n_s, 3, 6, length), jnp.float32),
                pltpu.VMEM((3, 40, length), jnp.float32),
                pltpu.VMEM((n_t, n_s, 6, length), jnp.float32),
                pltpu.VMEM((n_t + 1, n_s, 6, length), jnp.float32),
                pltpu.VMEM((n_t, n_s, 6, length), jnp.float32),
                pltpu.VMEM((n_s, 6, length), jnp.float32),
                pltpu.VMEM((2, 6, length), jnp.float32),
                pltpu.VMEM((total, total // CLUSTER), jnp.bfloat16),
                dma((n_s,)), dma((n_s,)),
                dma((n_s,)), dma((n_s,)),
                dma((n_s,)), dma((n_s,)),
                dma((n_t,)), dma((n_t,)),
                dma((n_s,)), dma((n_s,)),
                dma, dma,
            ],
            compiler_params=pltpu.CompilerParams(collective_id=0, has_side_effects=True),
        )(start_state, fine_nodes)

    return jax.shard_map(
        shards,
        mesh=mesh,
        in_specs=(P(None, "space"), P("tm", None, None, "space")),
        out_specs=(
            P("tm", None, None, "space"),
            P("tm", None, None, "space"),
            P("tm", None, "space"),
            P("tm", None, "space"),
        ),
        check_vma=False,
    )
```

time: 321 us -> 59.6 us (0.19)
  blocking collectives: 185 us -> 0 us
  other arithmetic: 71.9 us -> 0 us
  Pallas kernels: 0 us -> 53.8 us
  waiting for transfers between devices: 35 us -> 0 us
  starting transfers between devices: 17.2 us -> 0 us
  local copies, waits for them, and re-layouts: 8.51 us -> 4.6 us
    all_gather x14 -> x0, blocking collectives: 185 us -> none  [the longest x8 106 us: state_section(): sources = lax.all_gather(aggregate(initial), 'space', axis=1, tiled=True)]
    reduce_sum x53 -> x0, other arithmetic: 64.9 us -> none  [the longest x31 62.7 us: tile_sums(): jnp.sum(along * curl_x, axis=1)]
    pallas_call x0 -> x1, Pallas kernels: none -> 53.8 us  [shards(): pl.pallas_call(functools.partial(kernel, n_t, n_s), out_shape=(jax.ShapeD...]
    ppermute x9 -> x0, waiting for transfers between devices: 35 us -> none  [from_behind(): return lax.ppermute(block, axis, route)]
    ppermute x9 -> x0, starting transfers between devices: 17.2 us -> none  [from_behind(): return lax.ppermute(block, axis, route)]
    add x50 -> x0, other arithmetic: 6.13 us -> none  [the longest x8 4.98 us: state_section(): initial + step_length * (coarse_start + 0.5 * (coarse_last - coarse_first))]
    slice x86 -> x0, local copies, waits for them, and re-layouts: 4.36 us -> none  [the longest x11 1.06 us: aggregate(): grouped[3:6]]
  transfers between devices with their start and end apart: 9 -> 0, of which waited for: 9 -> 0; matrix products, arithmetic and copies ran while one was open for 0% -> 0% of each run, Pallas kernels for 0% -> 0%
where the time goes in v1:
time: 59.6 us; the launch traced here: 59 us
  Pallas kernels  53.8 us (90%)
  local copies, waits for them, and re-layouts  4.6 us (8%)
  between operations  0.66 us (1%)
    pallas_call x1, Pallas kernels, shards(): pl.pallas_call(functools.partial(kernel, n_t, n_s), out_shape=(jax.ShapeD...  53.8 us
    pallas_call x4, local copies, waits for them, and re-layouts, shards(): pl.pallas_call(functools.partial(kernel, n_t, n_s), out_shape=(jax.ShapeD...  3.2 us
    unnamed x7, local copies, waits for them, and re-layouts  1.4 us

profile of v1, /device:TPU:4, one launch (start us, length us, event | category | flops | bytes accessed | tf_op | source)
XLA Modules:
  0.0 59.0 jit_solution(14659173673881688178)
XLA Ops:
  0.6 1.4 %copy.6.nodes_ref = f32[1,3,6,512]{3,2,1,0:T(8,128)} copy(f32[1,3,6,512]{3,0,2,1:T(1,128)} %param.3) | data formatting | bytes 73728 | tf_op args[1]
  2.0 53.8 %shard_map.57 = (f32[1,3,3,512]{3,2,1,0:T(4,128)}, f32[1,3,3,512]{3,2,1,0:T(4,128)}, f32[1,3,512]{2,1,0:T(4,128)}, f32[1,3,512]{2,1,0:T(4,128)}) custom-call(f32[6,512]{1,0:T(8,128)} %start_ref.1, f32[1,3,6,512]{3,2,1,0:T(8,128)} %copy.6.nodes_ref), custom_call_target="tpu_custom_call" | custom-call | tf_op jit(solution)/shard_map/pallas_call | solution.py:399
  55.8 0.0 copy-start.2
  55.8 0.0 copy-start.1
  55.8 1.4 %copy.7 = f32[1,3,3,512]{3,0,2,1:T(1,128)} copy(f32[1,3,3,512]{3,2,1,0:T(4,128)} %get-tuple-element.4) | data formatting | bytes 36864 | tf_op jit(solution)/shard_map/pallas_call | solution.py:399
  57.2 0.0 copy-done.2
  57.2 0.0 copy-start
  57.2 0.6 %copy.9 = f32[1,3,512]{2,0,1:T(1,128)} copy(f32[1,3,512]{2,1,0:T(4,128)S(1)} %copy-done.2) | data formatting | bytes 12288 | tf_op jit(solution)/shard_map/pallas_call | solution.py:399
  57.8 0.0 copy-done.1
  57.8 0.6 %copy.10 = f32[1,3,512]{2,0,1:T(1,128)} copy(f32[1,3,512]{2,1,0:T(4,128)S(1)} %copy-done.1) | data formatting | bytes 12288 | tf_op jit(solution)/shard_map/pallas_call | solution.py:399
  58.4 0.0 copy-done
  58.4 0.6 %copy.8 = f32[1,3,3,512]{3,0,2,1:T(1,128)} copy(f32[1,3,3,512]{3,2,1,0:T(4,128)S(1)} %copy-done) | data formatting | bytes 36864 | tf_op jit(solution)/shard_map/pallas_call | solution.py:399
Async XLA Ops:
  55.8 1.4 %copy-start.2 = (f32[1,3,512]{2,1,0:T(4,128)S(1)}, f32[1,3,512]{2,1,0:T(4,128)}, u32[]{:S(2)}) copy-start(f32[1,3,512]{2,1,0:T(4,128)} %get-tuple-element.6) | copy-start | bytes 18436
  55.8 2.0 %copy-start.1 = (f32[1,3,512]{2,1,0:T(4,128)S(1)}, f32[1,3,512]{2,1,0:T(4,128)}, u32[]{:S(2)}) copy-start(f32[1,3,512]{2,1,0:T(4,128)} %get-tuple-element.7) | copy-start | bytes 18436
  57.2 1.2 %copy-start = (f32[1,3,3,512]{3,2,1,0:T(4,128)S(1)}, f32[1,3,3,512]{3,2,1,0:T(4,128)}, u32[]{:S(2)}) copy-start(f32[1,3,3,512]{3,2,1,0:T(4,128)} %get-tuple-element.5) | copy-start | bytes 55300

commit v2 on v1

--- a/solution.py
+++ b/solution.py
@@ -87,10 +87,10 @@
 def source_moments(state):
     base = pad_rows(jnp.concatenate([state[3:6], cross(state[0:3], state[3:6])], axis=0))
     whole = jnp.concatenate([base, state[0:1] * base, state[1:2] * base, state[2:3] * base], axis=0)
-    high = rounded(whole)
-    low = whole - high
-    for_q = jnp.concatenate([high[0:8], low[0:8]], axis=0).astype(jnp.bfloat16)
-    for_h = jnp.concatenate([high, low], axis=0).astype(jnp.bfloat16)
+    parts = split_three(whole)
+    for_q = jnp.concatenate([part[0:8] for part in parts] + [jnp.zeros_like(base)], axis=0)
+    for_q = for_q.astype(jnp.bfloat16)
+    for_h = jnp.concatenate(parts, axis=0).astype(jnp.bfloat16)
     return for_q, for_h
 
 
@@ -111,11 +111,12 @@
         steep = factor * square
         factor_high, factor_low = split_two(factor)
         steep_high, steep_low = split_two(steep)
-        got_q = product(for_q[:, part], factor_high) + product(for_q[:, part], factor_low)
+        got_q = product(for_q[:, part], factor_high)
+        low_q = product(for_q[0:16, part], factor_low)
         got_h = product(for_h[:, part], steep_high)
         low_h = product(for_h[0:32, part], steep_low)
-        sum_q = sum_q + (got_q[0:8] + got_q[8:16])
-        sum_h = sum_h + (got_h[0:32] + got_h[32:64] + low_h)
+        sum_q = sum_q + (got_q[0:8] + (got_q[8:16] + (got_q[16:24] + low_q[0:8])))
+        sum_h = sum_h + (got_h[0:32] + (got_h[32:64] + (got_h[64:96] + low_h)))
     return jnp.concatenate([sum_q, sum_h], axis=0)
 
 
@@ -184,6 +185,16 @@
             device_id={"tm": peer}, device_id_type=pl.DeviceIdType.MESH,
         )
 
+    lanes = nodes_ref.shape[1]
+    pieces = length // lanes
+
+    def put(target, row, value):
+        for one in range(value.shape[0]):
+            for piece in range(pieces):
+                target[row + one, piece : piece + 1, :] = value[
+                    one : one + 1, piece * lanes : (piece + 1) * lanes
+                ]
+
     barrier = pltpu.get_barrier_semaphore()
     for offset in range(1, n_s):
         pl.semaphore_signal(
@@ -195,11 +206,18 @@
             barrier, inc=1, device_id={"tm": lax.rem(mine + offset, n_t)},
             device_id_type=pl.DeviceIdType.MESH,
         )
+    for node in range(3):
+        for row in range(6):
+            for piece in range(pieces):
+                at = (node * 6 + row) * pieces + piece
+                gathered[me, node, row : row + 1, piece * lanes : (piece + 1) * lanes] = nodes_ref[
+                    at : at + 1, :
+                ]
     pl.semaphore_wait(barrier, n_s - 1 + n_t - 1)
 
     def node_copy(offset, slot):
         return space_copy(
-            nodes_ref.at[0], gathered.at[slot], send_a.at[offset], recv_a.at[offset],
+            gathered.at[me], gathered.at[slot], send_a.at[offset], recv_a.at[offset],
             lax.rem(me + offset, n_s),
         )
 
@@ -213,7 +231,6 @@
         node_copy(offset, me).start()
     for offset in range(1, n_s):
         start_copy(offset, me).start()
-    gathered[me] = nodes_ref[0]
     history[0, me] = start_ref[...]
 
     total = n_s * length
@@ -244,7 +261,7 @@
             node_copy(offset, source).wait_recv()
 
         def one_node(node, carry):
-            got = fine_sums(gathered[source, node], nodes_ref[0, node])
+            got = fine_sums(gathered[source, node], gathered[me, node])
             if offset == 0:
                 sums[node] = got
             else:
@@ -253,13 +270,13 @@
 
         lax.fori_loop(0, 3, one_node, 0)
 
-    fine = [finish(sums[node], nodes_ref[0, node], coupling) for node in range(3)]
+    fine = [finish(sums[node], gathered[me, node], coupling) for node in range(3)]
 
     def coarse_value(blocks, target):
         return finish(pair_sums(*coarse_sources(blocks), target_places(target)), target, coupling)
 
-    coarse_first = coarse_value([gathered[z, 0] for z in range(n_s)], nodes_ref[0, 0])
-    coarse_last = coarse_value([gathered[z, 2] for z in range(n_s)], nodes_ref[0, 2])
+    coarse_first = coarse_value([gathered[z, 0] for z in range(n_s)], gathered[me, 0])
+    coarse_last = coarse_value([gathered[z, 2] for z in range(n_s)], gathered[me, 2])
     correction = step_length * (
         (fine[0] + 4.0 * fine[1] + fine[2]) / 6.0 - 0.5 * (coarse_first + coarse_last)
     )
@@ -338,10 +355,10 @@
 
     for offset in range(1, n_s):
         middle_copy(offset, me).start()
-    places_out[0, 0] = initial[0:3]
-    strengths_out[0, 0] = initial[3:6]
-    places_out[0, 1] = sweep_middle[0:3]
-    strengths_out[0, 1] = sweep_middle[3:6]
+    put(places_out, 0, initial[0:3])
+    put(strengths_out, 0, initial[3:6])
+    put(places_out, 3, sweep_middle[0:3])
+    put(strengths_out, 3, sweep_middle[3:6])
     sums[1] = fine_sums(sweep_middle, sweep_middle)
     for offset in range(1, n_s):
         source = lax.rem(me + n_s - offset, n_s)
@@ -353,7 +370,7 @@
         + 0.5 * step_length * (slope_middle - fixed_middle)
         + step_length * (-fixed_first + 8.0 * fixed_middle + 5.0 * fixed_last) / 24.0
     )
-    handed[0] = sweep_last
+    put(handed.at[0], 0, sweep_last)
 
     def last_copy():
         return time_copy(handed.at[0], handed.at[1], send_h, recv_h, lax.rem(mine + 1, n_t))
@@ -362,8 +379,8 @@
     def _():
         last_copy().start()
 
-    places_out[0, 2] = sweep_last[0:3]
-    strengths_out[0, 2] = sweep_last[3:6]
+    places_out[6:9] = handed[0, 0:3]
+    strengths_out[6:9] = handed[0, 3:6]
     for offset in range(1, n_s):
         node_copy(offset, me).wait_send()
         start_copy(offset, me).wait_send()
@@ -374,14 +391,14 @@
 
     @pl.when(mine == 0)
     def _():
-        next_places_out[0] = start_ref[0:3]
-        next_strengths_out[0] = start_ref[3:6]
+        put(next_places_out, 0, start_ref[0:3])
+        put(next_strengths_out, 0, start_ref[3:6])
 
     @pl.when(mine > 0)
     def _():
         last_copy().wait_recv()
-        next_places_out[0] = handed[1, 0:3]
-        next_strengths_out[0] = handed[1, 3:6]
+        next_places_out[...] = handed[1, 0:3]
+        next_strengths_out[...] = handed[1, 3:6]
 
     @pl.when(mine < n_t - 1)
     def _():
@@ -396,13 +413,15 @@
         total = length * n_s
         vmem = pl.BlockSpec(memory_space=pltpu.VMEM)
         dma = pltpu.SemaphoreType.DMA
-        return pl.pallas_call(
+        lanes = math.gcd(length, 128)
+        rows = (length // lanes, lanes)
+        results = pl.pallas_call(
             functools.partial(kernel, n_t, n_s),
             out_shape=(
-                jax.ShapeDtypeStruct((1, 3, 3, length), jnp.float32),
-                jax.ShapeDtypeStruct((1, 3, 3, length), jnp.float32),
-                jax.ShapeDtypeStruct((1, 3, length), jnp.float32),
-                jax.ShapeDtypeStruct((1, 3, length), jnp.float32),
+                jax.ShapeDtypeStruct((9,) + rows, jnp.float32),
+                jax.ShapeDtypeStruct((9,) + rows, jnp.float32),
+                jax.ShapeDtypeStruct((3,) + rows, jnp.float32),
+                jax.ShapeDtypeStruct((3,) + rows, jnp.float32),
             ),
             in_specs=[vmem, vmem],
             out_specs=(vmem, vmem, vmem, vmem),
@@ -413,7 +432,7 @@
                 pltpu.VMEM((n_t + 1, n_s, 6, length), jnp.float32),
                 pltpu.VMEM((n_t, n_s, 6, length), jnp.float32),
                 pltpu.VMEM((n_s, 6, length), jnp.float32),
-                pltpu.VMEM((2, 6, length), jnp.float32),
+                pltpu.VMEM((2, 6) + rows, jnp.float32),
                 pltpu.VMEM((total, total // CLUSTER), jnp.bfloat16),
                 dma((n_s,)), dma((n_s,)),
                 dma((n_s,)), dma((n_s,)),
@@ -423,7 +442,11 @@
                 dma, dma,
             ],
             compiler_params=pltpu.CompilerParams(collective_id=0, has_side_effects=True),
-        )(start_state, fine_nodes)
+        )(start_state, fine_nodes.reshape(-1, lanes))
+        nodes, ends = (1, 3, 3, length), (1, 3, length)
+        return tuple(
+            one.reshape(shape) for one, shape in zip(results, (nodes, nodes, ends, ends))
+        )
 
     return jax.shard_map(
         shards,

time: 59.6 us -> 57.8 us (0.970)
  local copies, waits for them, and re-layouts: 4.6 us -> 3.33 us
  Pallas kernels: 53.8 us -> 53.2 us
    pallas_call x4 -> x0, local copies, waits for them, and re-layouts: 3.2 us -> none  [shards(): pl.pallas_call(functools.partial(kernel, n_t, n_s), out_shape=(jax.ShapeD...]
    unnamed x7 -> x10, local copies, waits for them, and re-layouts: 1.4 us -> 3.33 us
where the time goes in v2:
time: 57.8 us; the launch traced here: 57.1 us
  Pallas kernels  53.2 us (92%)
  local copies, waits for them, and re-layouts  3.33 us (6%)
  between operations  0.65 us (1%)
    pallas_call x1, Pallas kernels, shards(): pl.pallas_call(functools.partial(kernel, n_t, n_s), out_shape=(jax.ShapeD...  53.2 us
    unnamed x10, local copies, waits for them, and re-layouts  3.33 us

profile of v2, /device:TPU:4, one launch (start us, length us, event | category | flops | bytes accessed | tf_op | source)
XLA Modules:
  0.0 57.1 jit_solution(8875892955968554549)
XLA Ops:
  0.6 53.2 %shard_map.57 = (f32[9,4,128]{2,1,0:T(4,128)}, f32[9,4,128]{2,1,0:T(4,128)}, f32[3,4,128]{2,1,0:T(4,128)}, f32[3,4,128]{2,1,0:T(4,128)}) custom-call(f32[6,512]{1,0:T(8,128)} %start_ref.1, f32[72,128]{1,0:T(8,128)} %bitcast.5), custom_call_target="tpu_custom_call" | custom-call | tf_op jit(solution)/shard_map/pallas_call | solution.py:418
  53.8 0.0 copy-start
  53.8 1.3 %copy.18 = f32[1,3,3,512]{3,0,2,1:T(1,128)} copy(f32[1,3,3,512]{3,0,2,1:T(1,128)} %bitcast.7) | data formatting | bytes 36864
  55.2 0.0 copy-done
  55.2 0.0 copy-start.2
  55.2 0.6 %copy.19 = f32[1,3,3,512]{3,0,2,1:T(1,128)} copy(f32[1,3,3,512]{3,0,2,1:T(1,128)S(1)} %bitcast.6) | data formatting | bytes 36864
  55.8 0.1 copy-done.2
  55.9 0.0 copy-start.1
  55.9 0.6 %copy.20 = f32[1,3,512]{2,0,1:T(1,128)} copy(f32[1,3,512]{2,0,1:T(1,128)S(1)} %bitcast.9) | data formatting | bytes 12288
  56.5 0.1 copy-done.1
  56.6 0.6 %copy.21 = f32[1,3,512]{2,0,1:T(1,128)} copy(f32[1,3,512]{2,0,1:T(1,128)S(1)} %bitcast.8) | data formatting | bytes 12288
Async XLA Ops:
  53.8 1.3 %copy-start = (f32[9,4,128]{2,1,0:T(4,128)S(1)}, f32[9,4,128]{2,1,0:T(4,128)}, u32[]{:S(2)}) copy-start(f32[9,4,128]{2,1,0:T(4,128)} %get-tuple-element.9) | copy-start | bytes 55300
  55.2 0.7 %copy-start.2 = (f32[3,4,128]{2,1,0:T(4,128)S(1)}, f32[3,4,128]{2,1,0:T(4,128)}, u32[]{:S(2)}) copy-start(f32[3,4,128]{2,1,0:T(4,128)} %get-tuple-element.10) | copy-start | bytes 18436
  55.9 0.7 %copy-start.1 = (f32[3,4,128]{2,1,0:T(4,128)S(1)}, f32[3,4,128]{2,1,0:T(4,128)}, u32[]{:S(2)}) copy-start(f32[3,4,128]{2,1,0:T(4,128)} %get-tuple-element.11) | copy-start | bytes 18436

commit v3 on v2

--- a/solution.py
+++ b/solution.py
@@ -94,7 +94,7 @@
     return for_q, for_h
 
 
-def pair_sums(places, for_q, for_h, target):
+def pair_sums(places, for_q, for_h, target, both=True):
     count = target.shape[1]
     sum_q = jnp.zeros((8, count), jnp.float32)
     sum_h = jnp.zeros((32, count), jnp.float32)
@@ -112,11 +112,14 @@
         factor_high, factor_low = split_two(factor)
         steep_high, steep_low = split_two(steep)
         got_q = product(for_q[:, part], factor_high)
-        low_q = product(for_q[0:16, part], factor_low)
         got_h = product(for_h[:, part], steep_high)
-        low_h = product(for_h[0:32, part], steep_low)
-        sum_q = sum_q + (got_q[0:8] + (got_q[8:16] + (got_q[16:24] + low_q[0:8])))
-        sum_h = sum_h + (got_h[0:32] + (got_h[32:64] + (got_h[64:96] + low_h)))
+        rest_q = got_q[8:16] + got_q[16:24]
+        rest_h = got_h[32:64] + got_h[64:96]
+        if both:
+            rest_q = rest_q + product(for_q[0:16, part], factor_low)[0:8]
+            rest_h = rest_h + product(for_h[0:32, part], steep_low)
+        sum_q = sum_q + (got_q[0:8] + rest_q)
+        sum_h = sum_h + (got_h[0:32] + rest_h)
     return jnp.concatenate([sum_q, sum_h], axis=0)
 
 
@@ -251,9 +254,9 @@
         merged = aggregate(blocks)
         return (source_places(merged),) + source_moments(merged)
 
-    def fine_sums(source, target):
+    def fine_sums(source, target, both=True):
         for_q, for_h = source_moments(source)
-        return pair_sums(source_places(source), for_q, for_h, target_places(target))
+        return pair_sums(source_places(source), for_q, for_h, target_places(target), both)
 
     for offset in range(n_s):
         source = lax.rem(me + n_s - offset, n_s)
@@ -335,7 +338,7 @@
     sums[0] = jnp.zeros(sums.shape[1:], jnp.float32)
 
     def initial_block(z, carry):
-        sums[0] = sums[0] + fine_sums(history[mine, z], history[mine, me])
+        sums[0] = sums[0] + fine_sums(history[mine, z], history[mine, me], False)
         return carry
 
     lax.fori_loop(0, n_s, initial_block, 0)
@@ -359,11 +362,11 @@
     put(strengths_out, 0, initial[3:6])
     put(places_out, 3, sweep_middle[0:3])
     put(strengths_out, 3, sweep_middle[3:6])
-    sums[1] = fine_sums(sweep_middle, sweep_middle)
+    sums[1] = fine_sums(sweep_middle, sweep_middle, False)
     for offset in range(1, n_s):
         source = lax.rem(me + n_s - offset, n_s)
         middle_copy(offset, source).wait_recv()
-        sums[1] = sums[1] + fine_sums(middles[source], sweep_middle)
+        sums[1] = sums[1] + fine_sums(middles[source], sweep_middle, False)
     slope_middle = finish(sums[1], sweep_middle, coupling)
     sweep_last = (
         sweep_middle

time: 57.8 us -> 56.8 us (0.983)
  Pallas kernels: 53.2 us -> 52.2 us
    pallas_call x1, Pallas kernels: 53.2 us -> 52.2 us  [shards(): pl.pallas_call(functools.partial(kernel, n_t, n_s), out_shape=(jax.ShapeD...]
where the time goes in v3:
time: 56.8 us; the launch traced here: 56.1 us
  Pallas kernels  52.2 us (92%)
  local copies, waits for them, and re-layouts  3.33 us (6%)
  between operations  0.65 us (1%)
    pallas_call x1, Pallas kernels, shards(): pl.pallas_call(functools.partial(kernel, n_t, n_s), out_shape=(jax.ShapeD...  52.2 us
    unnamed x10, local copies, waits for them, and re-layouts  3.33 us

profile of v3, /device:TPU:4, one launch (start us, length us, event | category | flops | bytes accessed | tf_op | source)
XLA Modules:
  0.0 56.1 jit_solution(18227764595979536705)
XLA Ops:
  0.6 52.2 %shard_map.57 = (f32[9,4,128]{2,1,0:T(4,128)}, f32[9,4,128]{2,1,0:T(4,128)}, f32[3,4,128]{2,1,0:T(4,128)}, f32[3,4,128]{2,1,0:T(4,128)}) custom-call(f32[6,512]{1,0:T(8,128)} %start_ref.1, f32[72,128]{1,0:T(8,128)} %bitcast.5), custom_call_target="tpu_custom_call" | custom-call | tf_op jit(solution)/shard_map/pallas_call | solution.py:421
  52.8 0.0 copy-start
  52.8 1.3 %copy.18 = f32[1,3,3,512]{3,0,2,1:T(1,128)} copy(f32[1,3,3,512]{3,0,2,1:T(1,128)} %bitcast.7) | data formatting | bytes 36864
  54.1 0.0 copy-done
  54.1 0.0 copy-start.2
  54.1 0.6 %copy.19 = f32[1,3,3,512]{3,0,2,1:T(1,128)} copy(f32[1,3,3,512]{3,0,2,1:T(1,128)S(1)} %bitcast.6) | data formatting | bytes 36864
  54.8 0.1 copy-done.2
  54.8 0.0 copy-start.1
  54.8 0.6 %copy.20 = f32[1,3,512]{2,0,1:T(1,128)} copy(f32[1,3,512]{2,0,1:T(1,128)S(1)} %bitcast.9) | data formatting | bytes 12288
  55.4 0.1 copy-done.1
  55.5 0.6 %copy.21 = f32[1,3,512]{2,0,1:T(1,128)} copy(f32[1,3,512]{2,0,1:T(1,128)S(1)} %bitcast.8) | data formatting | bytes 12288
Async XLA Ops:
  52.8 1.3 %copy-start = (f32[9,4,128]{2,1,0:T(4,128)S(1)}, f32[9,4,128]{2,1,0:T(4,128)}, u32[]{:S(2)}) copy-start(f32[9,4,128]{2,1,0:T(4,128)} %get-tuple-element.9) | copy-start | bytes 55300
  54.1 0.7 %copy-start.2 = (f32[3,4,128]{2,1,0:T(4,128)S(1)}, f32[3,4,128]{2,1,0:T(4,128)}, u32[]{:S(2)}) copy-start(f32[3,4,128]{2,1,0:T(4,128)} %get-tuple-element.10) | copy-start | bytes 18436
  54.8 0.7 %copy-start.1 = (f32[3,4,128]{2,1,0:T(4,128)S(1)}, f32[3,4,128]{2,1,0:T(4,128)}, u32[]{:S(2)}) copy-start(f32[3,4,128]{2,1,0:T(4,128)} %get-tuple-element.11) | copy-start | bytes 18436
